TPU v7x, 32 devices: a whole 2x2x4 slice. The times are simulated.
32 devices in a mesh: dp: 8 (over y, x, core), tensor: 4 (over z).
Axes of the slice: x: 2, y: 2, z: 4, core: 2. Of those that a mesh axis runs over, the one named last changes fastest.
Arguments:
- hidden_in: bfloat16 [3, 4096, 768], P(None, ('dp', 'tensor')), may hold values from -6 to 6
- segment_ids: int32 [3, 32, 128], P(None, ('dp', 'tensor')), may hold values from 0 to 7, never falling along the last dimension, each value on 1 to 32 neighbouring positions
- pooled_grad: float32 [3, 32, 8, 768], P(None, ('dp', 'tensor')), may hold values from -96 to 96
- qkv_weight: bfloat16 [3, 768, 768], P(None, 'dp', 'tensor'), may hold values from -0.21875 to 0.21875
- qv_bias: bfloat16 [2, 768], P(None, ('dp', 'tensor')), may hold values from -1.1953125 to 1.1953125
- out_weight: bfloat16 [768, 768], P('tensor', 'dp'), may hold values from -0.875 to 0.875
- out_bias: bfloat16 [768], P(('dp', 'tensor')), may hold values from -1.1953125 to 1.1953125
- norm1_gain: bfloat16 [768], P(('dp', 'tensor')), may hold values from 0.099609375 to 1.8984375
- norm1_shift: bfloat16 [768], P(('dp', 'tensor')), may hold values from -1.1953125 to 1.1953125
- up_weight: bfloat16 [768, 3072], P('dp', 'tensor'), may hold values from -0.21875 to 0.21875
- up_bias: bfloat16 [3072], P(('dp', 'tensor')), may hold values from -1.1953125 to 1.1953125
- down_weight: bfloat16 [3072, 768], P('tensor', 'dp'), may hold values from -0.109375 to 0.109375
- down_bias: bfloat16 [768], P(('dp', 'tensor')), may hold values from -1.1953125 to 1.1953125
- norm2_gain: bfloat16 [768], P(('dp', 'tensor')), may hold values from 0.099609375 to 1.8984375
- norm2_shift: bfloat16 [768], P(('dp', 'tensor')), may hold values from -1.1953125 to 1.1953125
Outputs:
- pooled_out: float32 [3, 32, 8, 768], P(None, ('dp', 'tensor'))
- input_grad: float32 [3, 4096, 768], P(None, ('dp', 'tensor'))
- qkv_weight_grad: float32 [3, 768, 768], P(None, 'dp', 'tensor')
- qv_bias_grad: float32 [2, 768], P(None, ('dp', 'tensor'))
- out_weight_grad: float32 [768, 768], P('tensor', 'dp')
- out_bias_grad: float32 [768], P(('dp', 'tensor'))
- norm1_gain_grad: float32 [768], P(('dp', 'tensor'))
- norm1_shift_grad: float32 [768], P(('dp', 'tensor'))
- up_weight_grad: float32 [768, 3072], P('dp', 'tensor')
- up_bias_grad: float32 [3072], P(('dp', 'tensor'))
- down_weight_grad: float32 [3072, 768], P('tensor', 'dp')
- down_bias_grad: float32 [768], P(('dp', 'tensor'))
- norm2_gain_grad: float32 [768], P(('dp', 'tensor'))
- norm2_shift_grad: float32 [768], P(('dp', 'tensor'))
Inputs may be any that keep to these rules, and one draw needn't show every extreme that they name: `segment_ids`: in every row of 128 tokens the segment numbers never fall, each number from 0 to 7 occurs on 1 to 32 consecutive tokens, and some sentence has exactly 32 tokens.
All inputs are finite; a program needn't handle non-finite values.
Results may differ from a plain program's by a relative error of at most 0.013.
Values may be sent and summed in bfloat16 or wider, within the bound.
No kernel may reach another device: no remote copies, remote signals or barrier semaphores. Data moves between devices by JAX's collectives and lax.ppermute only.
A program may use at most 128 MiB of HBM per device.

v0:
```python
from functools import partial
import jax
import jax.numpy as jnp
from jax import lax
from jax.sharding import PartitionSpec as P

HD = 64
EPS = 1e-12
NEG = -1000000000.0
AXES = ("dp", "tensor")
f32 = jnp.float32
bf16 = jnp.bfloat16


def mm(spec, a, b):
    return jnp.einsum(spec, a, b, preferred_element_type=f32)


def normalize(values, gain, shift):
    center = values - jnp.mean(values, axis=-1, keepdims=True)
    inverse = lax.rsqrt(jnp.mean(center * center, axis=-1, keepdims=True) + EPS)
    normed = center * inverse
    return (normed * gain + shift, normed, inverse)


def normalize_back(grad_out, normed, inverse, gain):
    scaled = grad_out * gain
    return inverse * (
        scaled
        - jnp.mean(scaled, axis=-1, keepdims=True)
        - normed * jnp.mean(scaled * normed, axis=-1, keepdims=True)
    )


def per_device(
    hidden_in,
    segment_ids,
    pooled_grad,
    qkv_weight,
    qv_bias,
    out_weight,
    out_bias,
    norm1_gain,
    norm1_shift,
    up_weight,
    up_bias,
    down_weight,
    down_bias,
    norm2_gain,
    norm2_shift,
):
    n_dp, n_t = (lax.axis_size("dp"), lax.axis_size("tensor"))
    rows = qkv_weight.shape[1]
    hc = qkv_weight.shape[2]
    fc = up_weight.shape[1]
    D = rows * n_dp
    micro, tokens = (hidden_in.shape[0], hidden_in.shape[1])
    seqs, L = (segment_ids.shape[1], segment_ids.shape[2])
    G = micro * seqs
    T = micro * tokens
    segs = pooled_grad.shape[2]
    H = D // HD
    cols = 4 * hc + 2 * fc
    vecs = [
        qv_bias[0],
        qv_bias[1],
        out_bias,
        norm1_gain,
        norm1_shift,
        up_bias,
        down_bias,
        norm2_gain,
        norm2_shift,
    ]
    vlen = [v.shape[0] for v in vecs]
    vec = jnp.concatenate(vecs)
    main = jnp.concatenate(
        [qkv_weight[0], qkv_weight[1], qkv_weight[2], out_weight.T, up_weight, down_weight.T],
        axis=1,
    )
    full = lax.all_gather(main, "dp", axis=0, tiled=True)
    full = lax.all_gather(full, "tensor", axis=0)
    vfull = lax.all_gather(lax.all_gather(vec, "tensor"), "dp").reshape(n_dp * n_t, -1).astype(f32)

    def take(lo, width):
        return full[:, :, lo : lo + width].transpose(1, 0, 2).reshape(D, n_t * width)

    wq, wk, wv, wot = (take(c * hc, hc) for c in range(4))
    wu, wdt = (take(4 * hc, fc), take(4 * hc + fc, fc))
    offs = [0]
    for n in vlen:
        offs.append(offs[-1] + n)
    bq, bv, bo, g1, s1, bu, bd, g2, s2 = (
        vfull[:, offs[j] : offs[j + 1]].reshape(-1) for j in range(9)
    )
    x = hidden_in.reshape(T, D)
    seg = segment_ids.reshape(G, L)
    heads = (G, L, H, HD)
    q = (mm("rd,de->re", x, wq) + bq).astype(bf16).reshape(heads)
    k = mm("rd,de->re", x, wk).astype(bf16).reshape(heads)
    v = (mm("rd,de->re", x, wv) + bv).astype(bf16).reshape(heads)
    scale = float(HD) ** (-0.5)
    same = seg[:, None, :, None] == seg[:, None, None, :]
    s = jnp.where(same, mm("gqhd,gkhd->ghqk", q, k) * scale, NEG)
    e = jnp.exp(s - jnp.max(s, axis=-1, keepdims=True))
    pf = e / jnp.sum(e, axis=-1, keepdims=True)
    pb = pf.astype(bf16)
    o = mm("ghqk,gkhd->gqhd", pb, v).astype(bf16).reshape(T, D)
    a = mm("re,de->rd", o, wot) + bo + x.astype(f32)
    n1, x1, r1 = normalize(a, g1, s1)
    n1b = n1.astype(bf16)
    u = mm("rd,df->rf", n1b, wu) + bu
    z, pull = jax.vjp(partial(jax.nn.gelu, approximate=False), u)
    z = z.astype(bf16)
    b = mm("rf,df->rd", z, wdt) + bd + n1
    y, x2, r2 = normalize(b, g2, s2)
    onehot = (seg[:, :, None] == jnp.arange(segs, dtype=jnp.int32)).astype(f32)
    counts = jnp.sum(onehot, axis=1)
    hi = lax.Precision.HIGHEST
    pooled = (
        jnp.einsum("gls,gld->gsd", onehot, y.reshape(G, L, D), precision=hi) / counts[:, :, None]
    )
    dy = jnp.einsum(
        "gls,gsd->gld", onehot, pooled_grad.reshape(G, segs, D) / counts[:, :, None], precision=hi
    ).reshape(T, D)
    db = normalize_back(dy, x2, r2, g2)
    g_g2, g_s2, g_bd = (jnp.sum(dy * x2, 0), jnp.sum(dy, 0), jnp.sum(db, 0))
    dbb = db.astype(bf16)
    g_wdt = mm("rd,rf->df", dbb, z)
    du = pull(mm("rd,df->rf", dbb, wdt))[0].astype(bf16)
    g_wu = mm("rd,rf->df", n1b, du)
    g_bu = jnp.sum(du.astype(f32), 0)
    dn1 = mm("rf,df->rd", du, wu).astype(bf16).astype(f32) + db
    da = normalize_back(dn1, x1, r1, g1)
    g_g1, g_s1, g_bo = (jnp.sum(dn1 * x1, 0), jnp.sum(dn1, 0), jnp.sum(da, 0))
    dab = da.astype(bf16)
    g_wot = mm("rd,re->de", dab, o)
    do = mm("rd,de->re", dab, wot).astype(bf16).reshape(heads)
    dp = mm("gqhd,gkhd->ghqk", do, v)
    ds = (pf * (dp - jnp.sum(pf * dp, axis=-1, keepdims=True))).astype(bf16)
    dv = mm("ghqk,gqhd->gkhd", pb, do).astype(bf16).reshape(T, D)
    dq = (mm("ghqk,gkhd->gqhd", ds, k) * scale).astype(bf16).reshape(T, D)
    dk = (mm("ghqk,gqhd->gkhd", ds, q) * scale).astype(bf16).reshape(T, D)
    g_q, g_k, g_v = (mm("rd,re->de", x, dd) for dd in (dq, dk, dv))
    g_bq, g_bv = (jnp.sum(dq.astype(f32), 0), jnp.sum(dv.astype(f32), 0))
    dx = mm("re,de->rd", dq, wq) + mm("re,de->rd", dk, wk) + mm("re,de->rd", dv, wv) + da

    def blocks(g):
        return g.astype(bf16).reshape(D, n_t, -1).transpose(1, 0, 2)

    gfull = jnp.concatenate([blocks(g) for g in (g_q, g_k, g_v, g_wot, g_wu, g_wdt)], axis=2)
    gvec = jnp.concatenate(
        [g.reshape(n_dp * n_t, -1) for g in (g_bq, g_bv, g_bo, g_g1, g_s1, g_bu, g_bd, g_g2, g_s2)],
        axis=1,
    )
    gmine = lax.psum_scatter(gfull, "tensor", scatter_dimension=0)
    gmine = lax.psum_scatter(gmine, "dp", scatter_dimension=0, tiled=True).astype(f32)
    gv = lax.psum_scatter(gvec, AXES, scatter_dimension=0)
    vo = [gv[offs[j] : offs[j + 1]] for j in range(9)]
    return (
        pooled.reshape(micro, seqs, segs, D),
        dx.reshape(micro, tokens, D),
        jnp.stack([gmine[:, c * hc : (c + 1) * hc] for c in range(3)]),
        jnp.stack([vo[0], vo[1]]),
        gmine[:, 3 * hc : 4 * hc].T,
        vo[2],
        vo[3],
        vo[4],
        gmine[:, 4 * hc : 4 * hc + fc],
        vo[5],
        gmine[:, 4 * hc + fc :].T,
        vo[6],
        vo[7],
        vo[8],
    )


def solution(mesh):
    both = P(AXES)
    row3 = P(None, AXES)
    return jax.shard_map(
        per_device,
        mesh=mesh,
        in_specs=(
            row3,
            row3,
            row3,
            P(None, "dp", "tensor"),
            row3,
            P("tensor", "dp"),
            both,
            both,
            both,
            P("dp", "tensor"),
            both,
            P("tensor", "dp"),
            both,
            both,
            both,
        ),
        out_specs=(
            row3,
            row3,
            P(None, "dp", "tensor"),
            row3,
            P("tensor", "dp"),
            both,
            both,
            both,
            P("dp", "tensor"),
            both,
            P("tensor", "dp"),
            both,
            both,
            both,
        ),
        check_vma=False,
    )
```

profile of v0, /device:TPU:0, one launch (start us, length us, event | category | flops | bytes accessed | tf_op | source)
XLA Modules:
  0.0 762.0 jit_solution(15456504163924318695)
XLA Ops:
  10.9 36.8 %all-gather.7.cloned.1.call-done = bf16[768,2304]{1,0:T(8,128)(2,1)} async-done(((bf16[96,2304]{1,0:T(8,128)(2,1)}), bf16[768,2304]{1,0:T(8,128)(2,1)}) %all-gather.7.cloned.1.call-update) | async-done | bytes 3538960 | tf_op jit(solution)/shard_map/all_gather | solution.py:81
  50.1 11.7 %all-reduce = bf16[1152]{0:T(1024)(128)(2,1)S(1)} all-reduce(bf16[1152]{0:T(1024)(128)(2,1)S(1)} %dynamic-update-slice), channel_id=3, replica_groups=mesh['dp'=8,'tensor'=4] {'tensor'}, use_global_device_ids=true, to_apply=%add | all-reduce | flops 1152 | bytes 4608
  61.8 9.0 %all-gather.3 = bf16[8,4,288]{2,1,0:T(4,128)(2,1)S(1)} all-gather(bf16[1,4,288]{2,1,0:T(4,128)(2,1)S(1)} %reshape.268), channel_id=4, replica_groups=mesh['dp'=8,'tensor'=4] {'dp'}, dimensions={0}, use_global_device_ids=true | all-gather | bytes 20736 | tf_op jit(solution)/shard_map/all_gather | solution.py:83
  77.4 215.8 %all-gather.9.cloned.1.call-done = bf16[3072,2304]{1,0:T(8,128)(2,1)} async-done(((bf16[768,2304]{1,0:T(8,128)(2,1)}), bf16[3072,2304]{1,0:T(8,128)(2,1)}) %all-gather.9.cloned.1.call-update) | async-done | bytes 14155792 | tf_op jit(solution)/shard_map/all_gather | solution.py:82
  293.2 7.3 slice_bitcast_fusion.4
  300.5 7.9 %slice_bitcast_fusion = (bf16[768,4,768]{2,0,1:T(8,128)(2,1)}, bf16[768,4,768]{2,0,1:T(8,128)(2,1)}) fusion(bf16[4,768,2304]{2,1,0:T(8,128)(2,1)} %bitcast.194), kind=kLoop, calls=%fused_computation.7 | loop fusion | bytes 18874368 | tf_op jit(solution)/shard_map/transpose | solution.py:86
  308.4 6.6 copy.119
  317.7 2.9 fusion.22
  322.6 2.8 copy.117
  327.8 3.0 fusion.17
  345.6 6.7 copy.118
  352.3 14.5 %multiply_convert_fusion = (bf16[384,3072]{1,0:T(8,128)(2,1)S(1)}, f32[384,3072]{1,0:T(8,128)S(1)}, f32[384,3072]{1,0:T(8,128)S(1)}) fusion(f32[3072]{0:T(1024)} %add.126, bf16[768,3072]{0,1:T(8,128)(2,1)} %bitcast.201, f32[384,768]{1,0:T(8,128)S(1)} %get-tuple-element.119, f32[768]{0:T(1024)} %add.123, f32[768]{0:T(1024)S(1)} %mul.154, ...), kind=kOutput, calls=%fused_computation.11 | convolution fusion | flops 1891270656 | bytes 17716224 | tf_op jit(solution)/shard_map/rd,df->rf/dot_general | solution.py:16
  366.8 5.3 fusion.95
  375.6 7.6 convert_reduce_fusion
  383.2 2.9 multiply_reduce_fusion.1
  392.7 4.2 convert_reduce_fusion.1
  401.7 4.8 convolution_convert_fusion.1
  406.5 4.4 convolution_convert_fusion
  421.8 3.1 convolution_convert_fusion.4
  427.4 3.1 convolution_convert_fusion.5
  433.0 8.0 %bitcast_bitcast_fusion = (bf16[4,768,768]{2,1,0:T(8,128)(2,1)}, bf16[4,768,768]{2,1,0:T(8,128)(2,1)}) fusion(bf16[96,4,8,768]{3,2,1,0:T(8,128)(2,1)} %bitcast.207, bf16[96,4,8,768]{3,2,1,0:T(8,128)(2,1)} %bitcast.206), kind=kLoop, calls=%fused_computation.5 | loop fusion | bytes 18874368 | tf_op jit(solution)/shard_map/transpose | solution.py:149
  441.0 21.7 %concatenate.14 = bf16[4,768,2304]{2,1,0:T(8,128)(2,1)} concatenate(bf16[4,768,192]{2,1,0:T(8,128)(2,1)} %bitcast.198, bf16[4,768,192]{2,1,0:T(8,128)(2,1)} %bitcast.197, bf16[4,768,192]{2,1,0:T(8,128)(2,1)} %bitcast.196, bf16[4,768,192]{2,1,0:T(8,128)(2,1)S(1)} %bitcast.195, bf16[4,768,768]{2,1,0:T(8,128)(2,1)} %get-tuple-element.136, bf16[4,768,768]{2,1,0:T(8,128)(2,1)} %get-tuple-element.135), dimensions={2} | concatenate | bytes 28311552 | tf_op jit(solution)/shard_map/concatenate | solution.py:151
  462.8 235.5 %reduce-scatter.3.cloned.1.call-done = bf16[1,768,2304]{2,1,0:T(8,128)(2,1)} async-done(((bf16[4,768,2304]{2,1,0:T(8,128)(2,1)}), bf16[1,768,2304]{2,1,0:T(8,128)(2,1)}) %reduce-scatter.3.cloned.1.call-update) | async-done | bytes 3538960 | tf_op jit(solution)/shard_map/reduce_scatter | solution.py:156
  700.0 41.8 %all-reduce.1 = f32[32,288]{1,0:T(8,128)S(1)} all-reduce(f32[32,288]{1,0:T(8,128)S(1)} %concatenate.15), channel_id=7, replica_groups=mesh['dp'=8,'tensor'=4] {'dp','tensor'}, use_global_device_ids=true, to_apply=%region_23.24.clone | all-reduce | flops 9216 | bytes 73728
  (225 shorter events, 79.3 us)
Async XLA Ops:
  7.2 40.5 %all-gather.7.cloned.1.call-start = ((), (), s32[]{:S(2)}) async-start(), calls=%async_computation.2 | async-start | bytes 3981312 | tf_op jit(solution)/shard_map/all_gather | solution.py:81
  10.9 282.3 %all-gather.9.cloned.1.call-start = ((), (), s32[]{:S(2)}) async-start(), calls=%async_computation.5 | async-start | bytes 17694720 | tf_op jit(solution)/shard_map/all_gather | solution.py:82
  47.8 27.0 %copy-start.21 = (f32[3,1,8,768]{3,2,1,0:T(8,128)S(1)}, f32[3,1,8,768]{3,2,1,0:T(8,128)}, u32[]{:S(2)}) copy-start(f32[3,1,8,768]{3,2,1,0:T(8,128)} %param.17) | copy-start | bytes 221188
  47.8 650.5 %reduce-scatter.3.cloned.1.call-start = ((), (), s32[]{:S(2)}) async-start(), calls=%async_computation.3 | async-start | bytes 17694720 | tf_op jit(solution)/shard_map/reduce_scatter | solution.py:156
  71.8 294.9 %copy-start.29 = (f32[768]{0:T(1024)}, f32[768]{0:T(1024)S(1)}, u32[]{:S(2)}) copy-start(f32[768]{0:T(1024)S(1)} %mul.154) | copy-start | bytes 9220
  74.8 218.4 %copy-start.25 = (f32[3,8]{1,0:T(4,128)}, f32[3,8]{1,0:T(4,128)S(1)}, u32[]{:S(2)}) copy-start(f32[3,8]{1,0:T(4,128)S(1)} %convert_reduce_fusion.3) | copy-start | bytes 292
  322.6 15.7 %copy-start.7 = (bf16[3,128,12,64]{1,0,3,2:T(4,128)(2,1)}, bf16[3,128,12,64]{1,0,3,2:T(4,128)(2,1)S(1)}, u32[]{:S(2)}) copy-start(bf16[3,128,12,64]{1,0,3,2:T(4,128)(2,1)S(1)} %reshape.228) | copy-start | bytes 1769476
  344.6 41.5 %copy-start = (f32[384,768]{1,0:T(8,128)}, f32[384,768]{1,0:T(8,128)S(1)}, u32[]{:S(2)}) copy-start(f32[384,768]{1,0:T(8,128)S(1)} %get-tuple-element.119) | copy-start | bytes 3538948
  352.3 14.5 %copy-start.36 = (f32[384]{0:T(512)S(1)}, f32[384]{0:T(512)}, u32[]{:S(2)}) copy-start(f32[384]{0:T(512)} %add_rsqrt_fusion.1) | copy-start | bytes 4612
  352.3 14.5 %copy-start.40 = (f32[768]{0:T(1024)S(1)}, f32[768]{0:T(1024)}, u32[]{:S(2)}) copy-start(f32[768]{0:T(1024)} %add.123) | copy-start | bytes 9220
  352.3 14.5 %copy-start.44 = (f32[768]{0:T(1024)S(1)}, f32[768]{0:T(1024)}, u32[]{:S(2)}) copy-start(f32[768]{0:T(1024)} %add.129) | copy-start | bytes 9220
  366.8 5.3 copy-start.58
  373.5 9.7 %slice-start = ((s8[4718592]{0:T(1024)(128)(4,1)}), s8[4194304]{0:T(1024)(128)(4,1)S(1)}, s32[]{:S(2)}) async-start(s8[4718592]{0:T(1024)(128)(4,1)} %bitcast.202), calls=%async_computation.6 | async-start | bytes 8388608
  375.6 7.6 copy-start.18
  375.6 7.6 slice-start.1
  375.6 7.6 copy-start.30
  392.7 4.2 copy-start.13
  392.7 4.2 copy-start.20
  401.7 4.8 copy-start.19
  401.7 4.8 copy-start.59
  462.8 288.3 %reduce-scatter.5.cloned.1.call-start = ((), (), s32[]{:S(2)}) async-start(), calls=%async_computation.4 | async-start | bytes 3981312 | tf_op jit(solution)/shard_map/reduce_scatter | solution.py:157
  698.4 45.1 %copy-start.2 = (f32[384,768]{1,0:T(8,128)S(1)}, f32[384,768]{1,0:T(8,128)}, u32[]{:S(2)}) copy-start(f32[384,768]{1,0:T(8,128)} %get-tuple-element.90) | copy-start | bytes 3538948
  698.4 45.1 %copy-start.26 = (f32[3,8]{1,0:T(4,128)S(1)}, f32[3,8]{1,0:T(4,128)}, u32[]{:S(2)}) copy-start(f32[3,8]{1,0:T(4,128)} %copy-done.25) | copy-start | bytes 292
  751.1 3.5 copy-start.17
  (44 other events, 78.5 us)
Sparse Core Ops, SparseCore 0:
  11.0 36.6 all-gather.6
  49.3 243.9 all-gather.8
  462.9 235.4 reduce-scatter.2
  701.7 49.3 reduce-scatter.4
where the time goes:
time: 773 us; the launch traced here: 762 us
  waiting for transfers between devices  489 us (63%)
  local copies, waits for them, and re-layouts  105 us (14%)
  matrix products  79.7 us (10%)
  blocking collectives  62.4 us (8%)
  between operations  15.4 us (2%)
  other arithmetic  9.89 us (1%)
    reduce_scatter x1, waiting for transfers between devices, per_device(): gmine = lax.psum_scatter(gfull, 'tensor', scatter_dimension=0)  236 us
    all_gather x1, waiting for transfers between devices, per_device(): full = lax.all_gather(full, 'tensor', axis=0)  216 us
    dot_general x23, matrix products, mm(): return jnp.einsum(spec, a, b, preferred_element_type=f32)  74.8 us
    unnamed x2, blocking collectives  53.4 us
    transpose x8, local copies, waits for them, and re-layouts, take(): return full[:, :, lo:lo + width].transpose(1, 0, 2).reshape(D, n_t * width)  37.8 us
    all_gather x1, waiting for transfers between devices, per_device(): full = lax.all_gather(main, 'dp', axis=0, tiled=True)  36.8 us
    concatenate x1, local copies, waits for them, and re-layouts, per_device(): jnp.concatenate([blocks(g) for g in (g_q, g_k, g_v, g_wot, g_wu, g_wdt)],...  21.7 us
  transfers between devices with their start and end apart: 4, of which 4 were waited for; matrix products, arithmetic and copies ran while one was open for 2% of the time, Pallas kernels for 0%

commit v1 on v0

--- a/solution.py
+++ b/solution.py
@@ -78,7 +78,12 @@
         [qkv_weight[0], qkv_weight[1], qkv_weight[2], out_weight.T, up_weight, down_weight.T],
         axis=1,
     )
-    full = lax.all_gather(main, "dp", axis=0, tiled=True)
+    ring = [main]
+    for hop in range(7):
+        ring.append(lax.ppermute(ring[-1], "dp", [(dev, (dev + 1) % 8) for dev in range(8)]))
+    full = jnp.roll(
+        jnp.concatenate(ring[::-1], axis=0), (lax.axis_index("dp") + 1) * ring[0].shape[0], axis=0
+    )
     full = lax.all_gather(full, "tensor", axis=0)
     vfull = lax.all_gather(lax.all_gather(vec, "tensor"), "dp").reshape(n_dp * n_t, -1).astype(f32)
 

time: 773 us -> 794 us (1.027)
  waiting for transfers between devices: 489 us -> 512 us
    ppermute x0 -> x7, waiting for transfers between devices: none -> 60.6 us  [per_device(): lax.ppermute(ring[-1], 'dp', [(dev, (dev + 1) % 8) for dev in range(8)])]
    all_gather x1 -> x0, waiting for transfers between devices: 36.8 us -> none  [per_device(): full = lax.all_gather(main, 'dp', axis=0, tiled=True)]
  transfers between devices with their start and end apart: 4 -> 10, of which waited for: 4 -> 10; matrix products, arithmetic and copies ran while one was open for 2% -> 2% of each run, Pallas kernels for 0% -> 0%
where the time goes in v1:
time: 794 us; the launch traced here: 789 us
  waiting for transfers between devices  512 us (64%)
  local copies, waits for them, and re-layouts  108 us (14%)
  matrix products  79.6 us (10%)
  blocking collectives  63.8 us (8%)
  between operations  15.6 us (2%)
  other arithmetic  9.82 us (1%)
    reduce_scatter x1, waiting for transfers between devices, per_device(): gmine = lax.psum_scatter(gfull, 'tensor', scatter_dimension=0)  235 us
    all_gather x1, waiting for transfers between devices, per_device(): full = lax.all_gather(full, 'tensor', axis=0)  214 us
    dot_general x23, matrix products, mm(): return jnp.einsum(spec, a, b, preferred_element_type=f32)  74.7 us
    ppermute x7, waiting for transfers between devices, per_device(): lax.ppermute(ring[-1], 'dp', [(dev, (dev + 1) % 8) for dev in range(8)])  60.6 us
    unnamed x2, blocking collectives  54.5 us
    transpose x8, local copies, waits for them, and re-layouts, take(): return full[:, :, lo:lo + width].transpose(1, 0, 2).reshape(D, n_t * width)  37.7 us
    concatenate x1, local copies, waits for them, and re-layouts, per_device(): jnp.concatenate([blocks(g) for g in (g_q, g_k, g_v, g_wot, g_wu, g_wdt)],...  21.8 us
  transfers between devices with their start and end apart: 10, of which 10 were waited for; matrix products, arithmetic and copies ran while one was open for 2% of the time, Pallas kernels for 0%

profile of v1, /device:TPU:0, one launch (start us, length us, event | category | flops | bytes accessed | tf_op | source)
XLA Modules:
  0.0 789.4 jit_solution(1369196902616025391)
XLA Ops:
  10.6 8.9 %collective-permute-done = bf16[96,2304]{1,0:T(8,128)(2,1)S(1)} collective-permute-done((bf16[96,2304]{1,0:T(8,128)(2,1)S(1)}, bf16[96,2304]{1,0:T(8,128)(2,1)S(1)}, u32[]{:S(2)}, u32[]{:S(2)}) %collective-permute-start) | collective-permute-done | bytes 442400 | tf_op jit(solution)/shard_map/ppermute | solution.py:83
  19.5 8.6 %collective-permute-done.1 = bf16[96,2304]{1,0:T(8,128)(2,1)S(1)} collective-permute-done((bf16[96,2304]{1,0:T(8,128)(2,1)S(1)}, bf16[96,2304]{1,0:T(8,128)(2,1)S(1)}, u32[]{:S(2)}, u32[]{:S(2)}) %collective-permute-start.1) | collective-permute-done | bytes 442400 | tf_op jit(solution)/shard_map/ppermute | solution.py:83
  28.1 8.6 %collective-permute-done.2 = bf16[96,2304]{1,0:T(8,128)(2,1)S(1)} collective-permute-done((bf16[96,2304]{1,0:T(8,128)(2,1)S(1)}, bf16[96,2304]{1,0:T(8,128)(2,1)S(1)}, u32[]{:S(2)}, u32[]{:S(2)}) %collective-permute-start.2) | collective-permute-done | bytes 442400 | tf_op jit(solution)/shard_map/ppermute | solution.py:83
  36.7 8.6 %collective-permute-done.3 = bf16[96,2304]{1,0:T(8,128)(2,1)S(1)} collective-permute-done((bf16[96,2304]{1,0:T(8,128)(2,1)S(1)}, bf16[96,2304]{1,0:T(8,128)(2,1)S(1)}, u32[]{:S(2)}, u32[]{:S(2)}) %collective-permute-start.3) | collective-permute-done | bytes 442400 | tf_op jit(solution)/shard_map/ppermute | solution.py:83
  45.4 8.6 %collective-permute-done.4 = bf16[96,2304]{1,0:T(8,128)(2,1)S(1)} collective-permute-done((bf16[96,2304]{1,0:T(8,128)(2,1)S(1)}, bf16[96,2304]{1,0:T(8,128)(2,1)S(1)}, u32[]{:S(2)}, u32[]{:S(2)}) %collective-permute-start.4) | collective-permute-done | bytes 442400 | tf_op jit(solution)/shard_map/ppermute | solution.py:83
  54.0 8.6 %collective-permute-done.5 = bf16[96,2304]{1,0:T(8,128)(2,1)S(1)} collective-permute-done((bf16[96,2304]{1,0:T(8,128)(2,1)S(1)}, bf16[96,2304]{1,0:T(8,128)(2,1)S(1)}, u32[]{:S(2)}, u32[]{:S(2)}) %collective-permute-start.5) | collective-permute-done | bytes 442400 | tf_op jit(solution)/shard_map/ppermute | solution.py:83
  62.6 8.6 %collective-permute-done.6 = bf16[96,2304]{1,0:T(8,128)(2,1)S(1)} collective-permute-done((bf16[96,2304]{1,0:T(8,128)(2,1)S(1)}, bf16[96,2304]{1,0:T(8,128)(2,1)S(1)}, u32[]{:S(2)}, u32[]{:S(2)}) %collective-permute-start.6) | collective-permute-done | bytes 442400 | tf_op jit(solution)/shard_map/ppermute | solution.py:83
  76.8 12.7 %all-reduce = bf16[1152]{0:T(1024)(128)(2,1)S(1)} all-reduce(bf16[1152]{0:T(1024)(128)(2,1)S(1)} %dynamic-update-slice), channel_id=3, replica_groups=mesh['dp'=8,'tensor'=4] {'tensor'}, use_global_device_ids=true, to_apply=%add | all-reduce | flops 1152 | bytes 4608
  89.6 9.3 %all-gather.3 = bf16[8,4,288]{2,1,0:T(4,128)(2,1)S(1)} all-gather(bf16[1,4,288]{2,1,0:T(4,128)(2,1)S(1)} %reshape.268), channel_id=4, replica_groups=mesh['dp'=8,'tensor'=4] {'dp'}, dimensions={0}, use_global_device_ids=true | all-gather | bytes 20736 | tf_op jit(solution)/shard_map/all_gather | solution.py:88
  105.5 214.2 %all-gather.6.cloned.1.call-done = bf16[3072,2304]{1,0:T(8,128)(2,1)} async-done(((bf16[768,2304]{1,0:T(8,128)(2,1)}), bf16[3072,2304]{1,0:T(8,128)(2,1)}) %all-gather.6.cloned.1.call-update) | async-done | bytes 14155792 | tf_op jit(solution)/shard_map/all_gather | solution.py:87
  319.7 7.2 slice_bitcast_fusion.4
  327.0 7.9 %slice_bitcast_fusion = (bf16[768,4,768]{2,0,1:T(8,128)(2,1)}, bf16[768,4,768]{2,0,1:T(8,128)(2,1)}) fusion(bf16[4,768,2304]{2,1,0:T(8,128)(2,1)} %bitcast.194), kind=kLoop, calls=%fused_computation.7 | loop fusion | bytes 18874368 | tf_op jit(solution)/shard_map/transpose | solution.py:91
  334.9 6.7 copy.119
  371.9 6.6 copy.118
  378.5 14.5 %multiply_convert_fusion = (bf16[384,3072]{1,0:T(8,128)(2,1)S(1)}, f32[384,3072]{1,0:T(8,128)S(1)}, f32[384,3072]{1,0:T(8,128)S(1)}) fusion(f32[3072]{0:T(1024)} %add.142, bf16[768,3072]{0,1:T(8,128)(2,1)} %bitcast.201, f32[384,768]{1,0:T(8,128)S(1)} %get-tuple-element.119, f32[768]{0:T(1024)} %add.139, f32[768]{0:T(1024)S(1)} %mul.158, ...), kind=kOutput, calls=%fused_computation.11 | convolution fusion | flops 1891270656 | bytes 17716224 | tf_op jit(solution)/shard_map/rd,df->rf/dot_general | solution.py:16
  393.1 5.3 fusion.95
  401.9 7.6 convert_reduce_fusion
  419.0 4.2 convert_reduce_fusion.1
  428.0 4.8 convolution_convert_fusion.1
  432.8 4.4 convolution_convert_fusion
  460.4 8.0 %bitcast_bitcast_fusion = (bf16[4,768,768]{2,1,0:T(8,128)(2,1)}, bf16[4,768,768]{2,1,0:T(8,128)(2,1)}) fusion(bf16[96,4,8,768]{3,2,1,0:T(8,128)(2,1)} %bitcast.207, bf16[96,4,8,768]{3,2,1,0:T(8,128)(2,1)} %bitcast.206), kind=kLoop, calls=%fused_computation.5 | loop fusion | bytes 18874368 | tf_op jit(solution)/shard_map/transpose | solution.py:154
  468.4 21.8 %concatenate.21 = bf16[4,768,2304]{2,1,0:T(8,128)(2,1)} concatenate(bf16[4,768,192]{2,1,0:T(8,128)(2,1)} %bitcast.198, bf16[4,768,192]{2,1,0:T(8,128)(2,1)} %bitcast.197, bf16[4,768,192]{2,1,0:T(8,128)(2,1)} %bitcast.196, bf16[4,768,192]{2,1,0:T(8,128)(2,1)S(1)} %bitcast.195, bf16[4,768,768]{2,1,0:T(8,128)(2,1)} %get-tuple-element.136, bf16[4,768,768]{2,1,0:T(8,128)(2,1)} %get-tuple-element.135), dimensions={2} | concatenate | bytes 28311552 | tf_op jit(solution)/shard_map/concatenate | solution.py:156
  490.3 235.4 %reduce-scatter.3.cloned.1.call-done = bf16[1,768,2304]{2,1,0:T(8,128)(2,1)} async-done(((bf16[4,768,2304]{2,1,0:T(8,128)(2,1)}), bf16[1,768,2304]{2,1,0:T(8,128)(2,1)}) %reduce-scatter.3.cloned.1.call-update) | async-done | bytes 3538960 | tf_op jit(solution)/shard_map/reduce_scatter | solution.py:161
  726.7 41.8 %all-reduce.1 = f32[32,288]{1,0:T(8,128)S(1)} all-reduce(f32[32,288]{1,0:T(8,128)S(1)} %concatenate.22), channel_id=7, replica_groups=mesh['dp'=8,'tensor'=4] {'dp','tensor'}, use_global_device_ids=true, to_apply=%region_23.24.clone | all-reduce | flops 9216 | bytes 73728
  (251 shorter events, 100.8 us)
Async XLA Ops:
  7.2 312.5 %all-gather.6.cloned.1.call-start = ((), (), s32[]{:S(2)}) async-start(), calls=%async_computation.4 | async-start | bytes 17694720 | tf_op jit(solution)/shard_map/all_gather | solution.py:87
  10.1 9.4 %collective-permute-start = (bf16[96,2304]{1,0:T(8,128)(2,1)S(1)}, bf16[96,2304]{1,0:T(8,128)(2,1)S(1)}, u32[]{:S(2)}, u32[]{:S(2)}) collective-permute-start(bf16[96,2304]{1,0:T(8,128)(2,1)S(1)} %concatenate.18), channel_id=1, source_target_pairs={{0,4},{4,8},{8,12},{12,16},{16,20},{20,24},{24,28},{28,0},{1,5},{5... | collective-permute-start | bytes 1327112 | tf_op jit(solution)/shard_map/ppermute | solution.py:83
  19.5 8.6 %collective-permute-start.1 = (bf16[96,2304]{1,0:T(8,128)(2,1)S(1)}, bf16[96,2304]{1,0:T(8,128)(2,1)S(1)}, u32[]{:S(2)}, u32[]{:S(2)}) collective-permute-start(bf16[96,2304]{1,0:T(8,128)(2,1)S(1)} %collective-permute-done), channel_id=1, source_target_pairs={{0,4},{4,8},{8,12},{12,16},{16,20},{20,24},{24,28},{28,0},{1,5},{5... | collective-permute-start | bytes 1327112 | tf_op jit(solution)/shard_map/ppermute | solution.py:83
  28.1 8.6 %collective-permute-start.2 = (bf16[96,2304]{1,0:T(8,128)(2,1)S(1)}, bf16[96,2304]{1,0:T(8,128)(2,1)S(1)}, u32[]{:S(2)}, u32[]{:S(2)}) collective-permute-start(bf16[96,2304]{1,0:T(8,128)(2,1)S(1)} %collective-permute-done.1), channel_id=1, source_target_pairs={{0,4},{4,8},{8,12},{12,16},{16,20},{20,24},{24,28},{28,0},{1,5},{5... | collective-permute-start | bytes 1327112 | tf_op jit(solution)/shard_map/ppermute | solution.py:83
  36.7 8.6 %collective-permute-start.3 = (bf16[96,2304]{1,0:T(8,128)(2,1)S(1)}, bf16[96,2304]{1,0:T(8,128)(2,1)S(1)}, u32[]{:S(2)}, u32[]{:S(2)}) collective-permute-start(bf16[96,2304]{1,0:T(8,128)(2,1)S(1)} %collective-permute-done.2), channel_id=1, source_target_pairs={{0,4},{4,8},{8,12},{12,16},{16,20},{20,24},{24,28},{28,0},{1,5},{5... | collective-permute-start | bytes 1327112 | tf_op jit(solution)/shard_map/ppermute | solution.py:83
  45.3 8.6 %collective-permute-start.4 = (bf16[96,2304]{1,0:T(8,128)(2,1)S(1)}, bf16[96,2304]{1,0:T(8,128)(2,1)S(1)}, u32[]{:S(2)}, u32[]{:S(2)}) collective-permute-start(bf16[96,2304]{1,0:T(8,128)(2,1)S(1)} %collective-permute-done.3), channel_id=1, source_target_pairs={{0,4},{4,8},{8,12},{12,16},{16,20},{20,24},{24,28},{28,0},{1,5},{5... | collective-permute-start | bytes 1327112 | tf_op jit(solution)/shard_map/ppermute | solution.py:83
  54.0 8.6 %collective-permute-start.5 = (bf16[96,2304]{1,0:T(8,128)(2,1)S(1)}, bf16[96,2304]{1,0:T(8,128)(2,1)S(1)}, u32[]{:S(2)}, u32[]{:S(2)}) collective-permute-start(bf16[96,2304]{1,0:T(8,128)(2,1)S(1)} %collective-permute-done.4), channel_id=1, source_target_pairs={{0,4},{4,8},{8,12},{12,16},{16,20},{20,24},{24,28},{28,0},{1,5},{5... | collective-permute-start | bytes 1327112 | tf_op jit(solution)/shard_map/ppermute | solution.py:83
  62.6 8.6 %collective-permute-start.6 = (bf16[96,2304]{1,0:T(8,128)(2,1)S(1)}, bf16[96,2304]{1,0:T(8,128)(2,1)S(1)}, u32[]{:S(2)}, u32[]{:S(2)}) collective-permute-start(bf16[96,2304]{1,0:T(8,128)(2,1)S(1)} %collective-permute-done.5), channel_id=1, source_target_pairs={{0,4},{4,8},{8,12},{12,16},{16,20},{20,24},{24,28},{28,0},{1,5},{5... | collective-permute-start | bytes 1327112 | tf_op jit(solution)/shard_map/ppermute | solution.py:83
  74.5 28.4 %copy-start.20 = (f32[3,1,8,768]{3,2,1,0:T(8,128)S(1)}, f32[3,1,8,768]{3,2,1,0:T(8,128)}, u32[]{:S(2)}) copy-start(f32[3,1,8,768]{3,2,1,0:T(8,128)} %param.17) | copy-start | bytes 221188
  74.6 651.2 %reduce-scatter.3.cloned.1.call-start = ((), (), s32[]{:S(2)}) async-start(), calls=%async_computation.2 | async-start | bytes 17694720 | tf_op jit(solution)/shard_map/reduce_scatter | solution.py:161
  100.0 293.1 %copy-start.28 = (f32[768]{0:T(1024)}, f32[768]{0:T(1024)S(1)}, u32[]{:S(2)}) copy-start(f32[768]{0:T(1024)S(1)} %mul.158) | copy-start | bytes 9220
  102.9 216.8 %copy-start.24 = (f32[3,8]{1,0:T(4,128)}, f32[3,8]{1,0:T(4,128)S(1)}, u32[]{:S(2)}) copy-start(f32[3,8]{1,0:T(4,128)S(1)} %convert_reduce_fusion.3) | copy-start | bytes 292
  370.9 41.5 %copy-start = (f32[384,768]{1,0:T(8,128)}, f32[384,768]{1,0:T(8,128)S(1)}, u32[]{:S(2)}) copy-start(f32[384,768]{1,0:T(8,128)S(1)} %get-tuple-element.119) | copy-start | bytes 3538948
  490.2 235.6 %copy-start.26 = (f32[768]{0:T(1024)S(1)}, f32[768]{0:T(1024)}, u32[]{:S(2)}) copy-start(f32[768]{0:T(1024)} %get-tuple-element.75) | copy-start | bytes 9220
  490.2 235.7 %copy-start.34 = (f32[3072]{0:T(1024)S(1)}, f32[3072]{0:T(1024)}, u32[]{:S(2)}) copy-start(f32[3072]{0:T(1024)} %get-tuple-element.131) | copy-start | bytes 36868
  490.2 235.8 %copy-start.31 = (f32[768]{0:T(1024)S(1)}, f32[768]{0:T(1024)}, u32[]{:S(2)}) copy-start(f32[768]{0:T(1024)} %get-tuple-element.80) | copy-start | bytes 9220
  490.2 235.9 %copy-start.32 = (f32[768]{0:T(1024)S(1)}, f32[768]{0:T(1024)}, u32[]{:S(2)}) copy-start(f32[768]{0:T(1024)} %get-tuple-element.78) | copy-start | bytes 9220
  490.2 236.0 %copy-start.42 = (f32[768]{0:T(1024)S(1)}, f32[768]{0:T(1024)}, u32[]{:S(2)}) copy-start(f32[768]{0:T(1024)} %get-tuple-element.72) | copy-start | bytes 9220
  490.2 236.0 %copy-start.27 = (f32[768]{0:T(1024)S(1)}, f32[768]{0:T(1024)}, u32[]{:S(2)}) copy-start(f32[768]{0:T(1024)} %get-tuple-element.70) | copy-start | bytes 9220
  490.2 236.1 %copy-start.41 = (f32[768]{0:T(1024)S(1)}, f32[768]{0:T(1024)}, u32[]{:S(2)}) copy-start(f32[768]{0:T(1024)} %get-tuple-element.77) | copy-start | bytes 9220
  490.2 236.2 %copy-start.38 = (f32[12,64]{1,0:T(8,128)S(1)}, f32[12,64]{1,0:T(8,128)}, u32[]{:S(2)}) copy-start(f32[12,64]{1,0:T(8,128)} %get-tuple-element.129) | copy-start | bytes 9220
  490.3 280.1 %copy-start.2 = (f32[384,768]{1,0:T(8,128)S(1)}, f32[384,768]{1,0:T(8,128)}, u32[]{:S(2)}) copy-start(f32[384,768]{1,0:T(8,128)} %get-tuple-element.90) | copy-start | bytes 3538948
  490.3 280.1 %copy-start.25 = (f32[3,8]{1,0:T(4,128)S(1)}, f32[3,8]{1,0:T(4,128)}, u32[]{:S(2)}) copy-start(f32[3,8]{1,0:T(4,128)} %copy-done.24) | copy-start | bytes 292
  490.3 288.2 %reduce-scatter.5.cloned.1.call-start = ((), (), s32[]{:S(2)}) async-start(), calls=%async_computation.3 | async-start | bytes 3981312 | tf_op jit(solution)/shard_map/reduce_scatter | solution.py:162
  (49 other events, 201.4 us)
Sparse Core Ops, SparseCore 0:
  74.7 244.9 all-gather.5
  490.3 235.4 reduce-scatter.2
  729.2 49.1 reduce-scatter.4
